TPU v7x, 32 devices: a whole 2x2x4 slice. The times are simulated.
32 devices in a mesh: group: 1, req: 4 (over z), head: 4 (over y, x), pool: 2 (over core).
Axes of the slice: x: 2, y: 2, z: 4, core: 2. Of those that a mesh axis runs over, the one named last changes fastest.
Arguments:
- queries: bfloat16 [192, 4096], P(('group', 'req'), 'head'), may hold values from -128 to 128
- new_entries: bfloat16 [192, 2, 4, 256], P(('group', 'req'), None, 'head'), may hold values from -6 to 6
- cache_pages: bfloat16 [4, 416, 16, 256], P('head', ('group', 'req', 'pool')), may hold values from -6 to 6
- page_table: int32 [192, 2, 1], P(('group', 'req'), 'pool'), may hold values from 0 to 51, as said below
- cached_length: int32 [192, 2], P(('group', 'req'), 'pool'), may hold values from 1 to 16, as said below
- leave_slots: int32 [32], P(('group', 'req', 'pool')), may hold values from 0 to 50, as said below
- arrive_slots: int32 [32], P(('group', 'req', 'pool')), may hold values from 0 to 51, as said below
- residual: bfloat16 [192, 2048], P(('group', 'req', 'head')), may hold values from -5 to 5
- norm_gain: float32 [2048], replicated, may hold values from 0.5 to 1.5
- output_weight: bfloat16 [4096, 2048], P(('head', 'pool')), may hold values from -0.25 to 0.25
- expert_choice: int32 [192, 8], P(('group', 'req', 'head')), may hold values from 0 to 15, all different within a row; in each aligned block of 12 rows (0 to 11, 12 to 23, ...) at most 12 rows name the same one
- route_weight: float32 [192, 8], P(('group', 'req', 'head')), may hold values from 0.2 to 1
- gate_up: bfloat16 [16, 2, 384, 2048], P(('req', 'head'), None, 'pool'), may hold values from -0.125 to 0.125
- down_weight: bfloat16 [16, 384, 2048], P(('req', 'head'), 'pool'), may hold values from -0.3125 to 0.3125
Outputs:
- decoded: bfloat16 [192, 2048], P(('group', 'req', 'head'), 'pool')
Inputs may be any that keep to these rules, and one draw needn't show every extreme that they name: `page_table`: within each block of one index of req and one pool, the 48 entries name distinct slots, none of them among that block's leave_slots. `leave_slots`: each block's 4 entries are distinct. `arrive_slots`: each block's 4 entries are distinct slots that its page table names. `cached_length`: in every block of 48 requests and each pool some request has 16. `expert_choice`: each row names 8 distinct experts; in each aligned block of 12 rows no expert is named more than 12 times, a bound that some block reaches.
All inputs are finite; a program needn't handle non-finite values.
Results may differ from a plain program's by a relative error of at most 0.023.
Values may be sent and summed in bfloat16 or wider, within the bound.
A program may use at most 64 MiB of HBM per device.

v0:
```python
import jax
import jax.numpy as jnp
from jax import lax
from jax.sharding import PartitionSpec as P


def swapped(value, axis, apart):
    mask = 2**apart
    pairs = [(source, source ^ mask) for source in range(lax.axis_size(axis))]
    return lax.ppermute(value, axis, pairs)


def combined_all(shard, axis, join):
    gathered = jax.tree.map(
        lambda a, kind: lax.all_gather(a.astype(kind), axis),
        shard,
        (jnp.bfloat16, jnp.bfloat16, jnp.bfloat16),
    )

    def take(source):
        return jax.tree.map(
            lambda a, own: lax.dynamic_index_in_dim(a, source, 0, False).astype(own.dtype),
            gathered,
            shard,
        )

    return lax.fori_loop(
        1, lax.axis_size(axis), lambda source, state: join(state, take(source)), take(0)
    )


def merge_parts(earlier, later):
    first_max, first_denominator, first_value = earlier
    second_max, second_denominator, second_value = later
    largest = jnp.maximum(first_max, second_max)
    first_scale = jnp.exp(first_max - largest)
    second_scale = jnp.exp(second_max - largest)
    denominator = first_denominator * first_scale + second_denominator * second_scale
    weighted = first_value * first_scale[..., None] + second_value * second_scale[..., None]
    return (largest, denominator, weighted)


def local(
    queries,
    new_entries,
    cache_pages,
    page_table,
    cached_length,
    leave_slots,
    arrive_slots,
    residual,
    norm_gain,
    output_weight,
    expert_choice,
    route_weight,
    gate_up,
    down_weight,
):
    batch_size = queries.shape[0]
    group_count = cache_pages.shape[0]
    head_dim = new_entries.shape[3] // 2
    group_size = queries.shape[1] // (group_count * head_dim)
    pool_index = lax.axis_index("pool")
    outgoing = cache_pages[:, leave_slots]
    arrived = swapped(outgoing, "pool", 0)
    current = cache_pages.at[:, arrive_slots].set(arrived)
    context = current[:, page_table[:, 0, :]]
    context = context.reshape(group_count, batch_size, -1, 2 * head_dim)
    context_keys = context[..., :head_dim]
    context_values = context[..., head_dim:]
    grouped_queries = queries.reshape(batch_size, group_count, group_size, head_dim)
    score_scale = head_dim ** (-0.5)
    attention_scores = (
        jnp.einsum(
            "bgqd,gbtd->bgqt", grouped_queries, context_keys, preferred_element_type=jnp.float32
        )
        * score_scale
    )
    positions = jnp.arange(context.shape[2], dtype=jnp.int32)
    valid_mask = positions[None, :] < cached_length
    attention_scores = jnp.where(valid_mask[:, None, None, :], attention_scores, -jnp.inf)
    fresh_scores = (
        jnp.einsum(
            "bgqd,bsgd->bgqs",
            grouped_queries,
            new_entries[..., :head_dim],
            preferred_element_type=jnp.float32,
        )
        * score_scale
    )
    fresh_scores = jnp.where(pool_index == 0, fresh_scores, -jnp.inf)
    largest = jnp.maximum(jnp.max(attention_scores, axis=-1), jnp.max(fresh_scores, axis=-1))
    local_weights = jnp.exp(attention_scores - largest[..., None])
    fresh_weights = jnp.exp(fresh_scores - largest[..., None])
    denominator = jnp.sum(local_weights, axis=-1) + jnp.sum(fresh_weights, axis=-1)
    weighted = jnp.einsum("bgqt,gbtd->bgqd", local_weights, context_values.astype(jnp.float32))
    weighted = weighted + jnp.einsum(
        "bgqs,bsgd->bgqd", fresh_weights, new_entries[..., head_dim:].astype(jnp.float32)
    )
    largest, denominator, weighted = combined_all(
        (largest, denominator, weighted), "pool", merge_parts
    )
    attended = (weighted / denominator[..., None]).reshape(batch_size, -1).astype(jnp.bfloat16)
    head_width = output_weight.shape[0]
    own_heads = lax.dynamic_slice_in_dim(attended, pool_index * head_width, head_width, 1)
    partial_value = jnp.dot(own_heads, output_weight, preferred_element_type=jnp.float32)
    rows_here = residual.shape[0]
    summed = lax.psum(partial_value.astype(jnp.bfloat16), ("head", "pool")).astype(jnp.float32)
    attention = lax.dynamic_slice_in_dim(summed, lax.axis_index("head") * rows_here, rows_here, 0)
    hidden = residual.astype(jnp.float32) + attention
    normed = (
        hidden * lax.rsqrt(jnp.mean(hidden * hidden, axis=-1, keepdims=True) + 1e-06) * norm_gain
    ).astype(jnp.bfloat16)
    expert_count = lax.axis_size("req") * lax.axis_size("head")
    top_count = expert_choice.shape[1]
    capacity = max(
        2, min(rows_here, (2 * rows_here * top_count + expert_count - 1) // expert_count)
    )
    flat_choice = expert_choice.reshape(-1)
    expert_hits = (
        flat_choice[:, None] == jnp.arange(expert_count, dtype=jnp.int32)[None, :]
    ).astype(jnp.int32)
    earlier = jnp.cumsum(expert_hits, axis=0) - expert_hits
    slot_index = jnp.sum(earlier * expert_hits, axis=1)
    target = flat_choice * capacity + slot_index
    placed = (
        target[:, None] == jnp.arange(expert_count * capacity, dtype=jnp.int32)[None, :]
    ).astype(jnp.float32)
    placed = placed.reshape(rows_here, top_count, expert_count * capacity)
    dispatch = jnp.sum(placed, axis=1).astype(jnp.bfloat16)
    combine_matrix = jnp.sum(placed * route_weight[:, :, None], axis=1)
    outgoing_rows = jnp.einsum("re,rd->ed", dispatch, normed, preferred_element_type=jnp.float32)
    outgoing_rows = outgoing_rows.astype(jnp.bfloat16).reshape(expert_count, capacity, -1)
    model_width = normed.shape[1]
    half_width = model_width // lax.axis_size("pool")
    projection = gate_up[0].reshape(-1, model_width)
    hidden_size = projection.shape[0] // 2
    received = lax.all_to_all(
        outgoing_rows, ("req", "head"), split_axis=0, concat_axis=0, tiled=True
    )
    sources = received.shape[0]
    item_count = received.shape[1]
    flat_rows = received.reshape(sources * item_count, model_width)
    projected = jnp.einsum("nd,fd->nf", flat_rows, projection, preferred_element_type=jnp.float32)
    activated = (jax.nn.silu(projected[:, :hidden_size]) * projected[:, hidden_size:]).astype(
        jnp.bfloat16
    )
    part_sum = jnp.dot(activated, down_weight[0], preferred_element_type=jnp.float32).reshape(
        sources, item_count, model_width
    )
    column_sum = lax.psum_scatter(
        part_sum.astype(jnp.bfloat16), "pool", scatter_dimension=2, tiled=True
    )
    returned = lax.all_to_all(column_sum, ("req", "head"), split_axis=0, concat_axis=0, tiled=True)
    gathered = returned.reshape(expert_count * capacity, half_width).astype(jnp.float32)
    expert_mix = jnp.dot(combine_matrix, gathered, precision=lax.Precision.HIGHEST)
    own_columns = lax.dynamic_slice_in_dim(hidden, pool_index * half_width, half_width, 1)
    return (own_columns + expert_mix).astype(jnp.bfloat16)


def solution(mesh):
    return jax.shard_map(
        local,
        mesh=mesh,
        in_specs=(
            P(("group", "req"), "head"),
            P(("group", "req"), None, "head", None),
            P("head", ("group", "req", "pool"), None, None),
            P(("group", "req"), "pool", None),
            P(("group", "req"), "pool"),
            P(("group", "req", "pool")),
            P(("group", "req", "pool")),
            P(("group", "req", "head"), None),
            P(),
            P(("head", "pool"), None),
            P(("group", "req", "head"), None),
            P(("group", "req", "head"), None),
            P(("req", "head"), None, "pool", None),
            P(("req", "head"), "pool", None),
        ),
        out_specs=P(("group", "req", "head"), "pool"),
        check_vma=False,
    )
```

profile of v0, /device:TPU:0, one launch (start us, length us, event | category | flops | bytes accessed | tf_op | source)
XLA Modules:
  0.0 159.7 jit_solution(2999815218880634779)
XLA Ops:
  6.5 1.2 copy.73
  7.7 0.7 compare_select_fusion.1
  8.4 0.5 gather_fusion
  8.9 0.6 collective-permute-start
  9.5 0.7 fusion.23
  10.2 0.7 compare_select_fusion.2
  10.8 0.7 iota_compare_fusion.2
  11.5 0.8 copy.59
  12.3 0.1 eq.33
  12.4 0.1 fusion.12
  12.5 0.1 reduce_window_sum.11
  12.6 0.2 select_reduce_fusion.1
  12.8 0.1 reduce_sum.59
  12.9 0.9 copy.64
  13.8 1.0 fusion.25
  14.8 0.1 copy.61
  14.9 0.6 scatter_fusion
  15.5 0.6 gather_fusion.1
  16.1 0.3 fusion.24
  16.4 0.1 fusion.14
  16.6 0.2 fusion.15
  16.8 0.1 copy.54
  16.9 1.8 %all-gather.3 = bf16[2,48,8]{1,2,0:T(8,128)(2,1)S(1)} all-gather(bf16[1,48,8]{1,2,0:T(8,128)(2,1)S(1)} %copy.54), channel_id=3, replica_groups=mesh['group'=1,'req'=4,'head'=4,'pool'=2] {'pool'}, dimensions={0}, use_global_device_ids=true | all-gather | bytes 2304 | tf_op jit(solution)/shard_map/all_gather | solution.py:15
  18.7 0.2 fusion.7
  19.0 1.8 %all-gather.4 = bf16[2,48,8]{1,2,0:T(8,128)(2,1)S(1)} all-gather(bf16[1,48,8]{1,2,0:T(8,128)(2,1)S(1)} %copy.57), channel_id=4, replica_groups=mesh['group'=1,'req'=4,'head'=4,'pool'=2] {'pool'}, dimensions={0}, use_global_device_ids=true | all-gather | bytes 2304 | tf_op jit(solution)/shard_map/all_gather | solution.py:15
  20.9 0.1 copy.55
  21.0 0.1 copy.58
  21.0 0.1 copy.56
  21.1 0.3 fusion.2
  21.4 1.9 %all-gather = bf16[96,8,128]{2,1,0:T(8,128)(2,1)S(1)} all-gather(bf16[48,8,128]{2,1,0:T(8,128)(2,1)S(1)} %fusion.2), channel_id=2, replica_groups=mesh['group'=1,'req'=4,'head'=4,'pool'=2] {'pool'}, dimensions={0}, use_global_device_ids=true | all-gather | bytes 294912 | tf_op jit(solution)/shard_map/all_gather | solution.py:15
  23.3 0.2 divide_convert_fusion
  23.6 1.2 convolution_convert_fusion.2
  24.8 0.1 convert_reduce_fusion
  25.0 56.1 %all-reduce.2.cloned.1.call-done = bf16[48,2048]{1,0:T(8,128)(2,1)} async-done(((bf16[48,2048]{1,0:T(8,128)(2,1)}), bf16[48,2048]{1,0:T(8,128)(2,1)}) %all-reduce.2.cloned.1.call-update) | async-done | bytes 196624 | tf_op jit(solution)/shard_map/psum | solution.py:108
  81.0 1.0 multiply_reduce_fusion
  82.1 1.3 convolution_convert_fusion.1
  83.4 1.3 reshape.273
  84.6 30.5 %all_to_all.10 = bf16[16,12,2048]{2,1,0:T(8,128)(2,1)} all-to-all(bf16[16,12,2048]{2,1,0:T(8,128)(2,1)S(1)} %reshape.273), channel_id=1, replica_groups=mesh['group'=1,'req'=4,'head'=4,'pool'=2] {'req','head'}, dimensions={0} | all-to-all | bytes 1572864 | tf_op jit(solution)/shard_map/all_to_all | solution.py:138
  115.1 1.3 reshape.274
  116.4 2.1 %fusion.26 = f32[192,384]{1,0:T(8,128)S(1)} fusion(bf16[192,2048]{1,0:T(8,128)(2,1)S(1)} %reshape.274, bf16[384,2048]{1,0:T(8,128)(2,1)} %bitcast.85), kind=kOutput, calls=%fused_computation.71 | convolution fusion | flops 301989888 | bytes 2654208 | tf_op jit(solution)/shard_map/nd,fd->nf/dot_general | solution.py:144
  118.5 0.1 fusion.6
  118.7 2.4 %convolution_convert_fusion = bf16[16,12,2048]{2,0,1:T(8,128)(2,1)} fusion(bf16[1,192,2048]{2,1,0:T(8,128)(2,1)} %param.27, bf16[16,12,192]{2,1,0:T(8,128)(2,1)S(1)} %dot_general.36), kind=kOutput, calls=%fused_computation.3 | convolution fusion | flops 151388160 | bytes 1646592 | tf_op jit(solution)/shard_map/dot_general | solution.py:148
  121.1 6.6 %reduce-scatter.2.cloned.1.call-done = bf16[16,12,1024]{2,0,1:T(8,128)(2,1)} async-done(((bf16[16,12,2048]{2,0,1:T(8,128)(2,1)}), bf16[16,12,1024]{2,0,1:T(8,128)(2,1)}) %reduce-scatter.2.cloned.1.call-update) | async-done | bytes 393232 | tf_op jit(solution)/shard_map/reduce_scatter | solution.py:151
  127.6 2.0 %copy.63 = bf16[16,12,1024]{2,1,0:T(8,128)(2,1)} copy(bf16[16,12,1024]{2,0,1:T(8,128)(2,1)} %reduce-scatter.2.cloned.1.call-done) | data formatting | bytes 786432 | tf_op jit(solution)/shard_map/reduce_scatter | solution.py:151
  129.6 6.7 %all-to-all-start.1 = ((bf16[16,12,1024]{2,1,0:T(8,128)(2,1)}), bf16[16,12,1024]{2,1,0:T(8,128)(2,1)S(1)}, u32[]{:S(2)}, u32[]{:S(2)}) async-start(bf16[16,12,1024]{2,1,0:T(8,128)(2,1)} %copy.63), calls=%async_computation.2 | async-start | bytes 1048576 | tf_op jit(solution)/shard_map/all_to_all | solution.py:154
  136.4 15.5 %all-to-all-done.1 = bf16[16,12,1024]{2,1,0:T(8,128)(2,1)S(1)} async-done(((bf16[16,12,1024]{2,1,0:T(8,128)(2,1)}), bf16[16,12,1024]{2,1,0:T(8,128)(2,1)S(1)}, u32[]{:S(2)}, u32[]{:S(2)}) %all-to-all-start.1) | async-done | bytes 393248 | tf_op jit(solution)/shard_map/all_to_all | solution.py:154
  151.9 0.1 reshape.275
  151.9 0.9 fusion.4
  (25 shorter events, 0.3 us)
Async XLA Ops:
  6.5 17.1 %copy-start = (bf16[512,2048]{1,0:T(8,128)(2,1)S(1)}, bf16[512,2048]{1,0:T(8,128)(2,1)}, u32[]{:S(2)}) copy-start(bf16[512,2048]{1,0:T(8,128)(2,1)} %param.23) | copy-start | bytes 6291460
  6.5 10.0 %copy-start.2 = (bf16[48,2,1,256]{3,1,2,0:T(2,128)(2,1)S(1)}, bf16[48,2,1,256]{3,1,2,0:T(2,128)(2,1)}, u32[]{:S(2)}) copy-start(bf16[48,2,1,256]{3,1,2,0:T(2,128)(2,1)} %param.15) | copy-start | bytes 147460
  6.5 8.3 %copy-start.4 = (f32[12,8]{0,1:T(8,128)S(1)}, f32[12,8]{0,1:T(8,128)}, u32[]{:S(2)}) copy-start(f32[12,8]{0,1:T(8,128)} %param.25) | copy-start | bytes 1156
  6.5 74.5 %all-reduce.2.cloned.1.call-start = ((), (), s32[]{:S(2)}) async-start(), calls=%async_computation.3 | async-start | bytes 393216 | tf_op jit(solution)/shard_map/psum | solution.py:108
  8.9 6.0 %collective-permute-start = (bf16[1,4,16,256]{3,2,1,0:T(8,128)(2,1)S(1)}, bf16[1,4,16,256]{3,2,1,0:T(8,128)(2,1)S(1)}, u32[]{:S(2)}, u32[]{:S(2)}) collective-permute-start(bf16[1,4,16,256]{3,2,1,0:T(8,128)(2,1)S(1)} %bitcast.94), channel_id=1, source_target_pairs={{0,1},{1,0},{2,3},{3,2},{4,5},{5,4},{6,7},{7,6},{8,9},{9,8},{10,11... | collective-permute-start | bytes 98312 | tf_op jit(solution)/shard_map/ppermute | solution.py:10
  23.3 57.7 %copy-start.1 = (bf16[12,2048]{1,0:T(8,128)(2,1)S(1)}, bf16[12,2048]{1,0:T(8,128)(2,1)}, u32[]{:S(2)}) copy-start(bf16[12,2048]{1,0:T(8,128)(2,1)} %param.21) | copy-start | bytes 147460
  23.6 58.5 %copy-start.3 = (f32[2048]{0:T(1024)S(1)}, f32[2048]{0:T(1024)}, u32[]{:S(2)}) copy-start(f32[2048]{0:T(1024)} %param.22) | copy-start | bytes 24580
  24.8 102.8 %reduce-scatter.2.cloned.1.call-start = ((), (), s32[]{:S(2)}) async-start(), calls=%async_computation.4 | async-start | bytes 1179648 | tf_op jit(solution)/shard_map/reduce_scatter | solution.py:151
  129.6 22.2 %all-to-all-start.1 = ((bf16[16,12,1024]{2,1,0:T(8,128)(2,1)}), bf16[16,12,1024]{2,1,0:T(8,128)(2,1)S(1)}, u32[]{:S(2)}, u32[]{:S(2)}) async-start(bf16[16,12,1024]{2,1,0:T(8,128)(2,1)} %copy.63), calls=%async_computation.2 | async-start | bytes 1048576 | tf_op jit(solution)/shard_map/all_to_all | solution.py:154
Sparse Core Ops, SparseCore 0:
  24.9 56.0 all-reduce.1
  121.2 6.3 reduce-scatter.1
where the time goes:
time: 160 us
  waiting for transfers between devices  78.1 us (49%)
  blocking collectives  36.1 us (23%)
  between operations  13.6 us (8%)
  local copies, waits for them, and re-layouts  10 us (6%)
  matrix products  9.56 us (6%)
  starting transfers between devices  7.33 us (5%)
  other arithmetic  4.95 us (3%)
    psum x1, waiting for transfers between devices, local(): lax.psum(partial_value.astype(jnp.bfloat16), ('head', 'pool'))  56.1 us
    all_to_all x1, blocking collectives, local(): lax.all_to_all(outgoing_rows, ('req', 'head'), split_axis=0, concat_axis=...  30.5 us
    all_to_all x1, waiting for transfers between devices, local(): lax.all_to_all(column_sum, ('req', 'head'), split_axis=0, concat_axis=0,...  15.5 us
    all_to_all x1, starting transfers between devices, local(): lax.all_to_all(column_sum, ('req', 'head'), split_axis=0, concat_axis=0,...  6.73 us
    reduce_scatter x1, waiting for transfers between devices, local(): lax.psum_scatter(part_sum.astype(jnp.bfloat16), 'pool', scatter_dimension...  6.55 us
    all_gather x3, blocking collectives, combined_all(): lax.all_gather(a.astype(kind), axis)  5.63 us
  transfers between devices with their start and end apart: 4, of which 3 were waited for; matrix products, arithmetic and copies ran while one was open for 3% of the time, Pallas kernels for 0%

commit v1 on v0

--- a/solution.py
+++ b/solution.py
@@ -1,7 +1,15 @@
+import functools
+
 import jax
 import jax.numpy as jnp
 from jax import lax
+from jax.experimental import pallas as pl
+from jax.experimental.pallas import tpu as pltpu
 from jax.sharding import PartitionSpec as P
+
+MESH = pl.DeviceIdType.MESH
+ROW_TILE = 16
+NEGATIVE = -1e30
 
 
 def swapped(value, axis, apart):
@@ -40,7 +48,7 @@
     return (largest, denominator, weighted)
 
 
-def local(
+def local_routed(
     queries,
     new_entries,
     cache_pages,
@@ -158,6 +166,534 @@
     return (own_columns + expert_mix).astype(jnp.bfloat16)
 
 
+def layer_kernel(
+    req_count,
+    head_count,
+    pool_count,
+    page_table,
+    leave_slots,
+    arrive_slots,
+    cached_length,
+    expert_choice,
+    route_weight,
+    residual,
+    norm_gain,
+    queries_hbm,
+    fresh_hbm,
+    cache_hbm,
+    output_weight_hbm,
+    gate_up_hbm,
+    down_weight_hbm,
+    decoded,
+    queries,
+    fresh,
+    cache,
+    output_weight,
+    gate_up,
+    down_weight,
+    leaving,
+    arrived,
+    context,
+    weights,
+    values_out,
+    values_in,
+    level_out,
+    level_in,
+    partial_out,
+    partial_in,
+    hidden,
+    active,
+    own_part,
+    pool_out,
+    pool_in,
+    head_out,
+    head_in,
+    totals,
+    req_out,
+    req_in,
+    load_sem,
+    send_sem,
+    recv_sem,
+):
+    r, h, p = lax.axis_index("req"), lax.axis_index("head"), lax.axis_index("pool")
+    batch, page = queries.shape[0], cache.shape[1]
+    head_dim = cache.shape[2] // 2
+    group_size = queries.shape[1] // head_dim
+    rows_here = residual.shape[0]
+    width = residual.shape[1]
+    col_block = width // (head_count * pool_count)
+    half = width // pool_count
+    half_heads = group_size // pool_count
+    chunks = batch // ROW_TILE
+    moves = leaving.shape[0]
+
+    loads = [
+        pltpu.make_async_copy(source, target, load_sem.at[i])
+        for i, (source, target) in enumerate(
+            (
+                (cache_hbm.at[0], cache),
+                (queries_hbm, queries),
+                (fresh_hbm.at[p], fresh),
+                (output_weight_hbm, output_weight),
+                (gate_up_hbm.at[0], gate_up),
+                (down_weight_hbm.at[0], down_weight),
+            )
+        )
+    ]
+    for load in loads:
+        load.start()
+
+    def req_peer(k):
+        return lax.rem(r + k, req_count)
+
+    def head_peer(k):
+        return lax.rem(h + k, head_count)
+
+    def req_source(k):
+        return lax.rem(r + req_count - k, req_count)
+
+    def head_source(k):
+        return lax.rem(h + head_count - k, head_count)
+
+    partner = 1 - p
+    barrier = pltpu.get_barrier_semaphore()
+    peers = [
+        (kr, kh, kp)
+        for kr in range(req_count)
+        for kh in range(head_count)
+        for kp in range(pool_count)
+        if (kr, kh, kp) != (0, 0, 0) and (kp == 0 or kr == 0)
+    ]
+
+    def where_is(kr, kh, kp):
+        return {
+            "req": req_peer(kr) if kr else r,
+            "head": head_peer(kh) if kh else h,
+            "pool": partner if kp else p,
+        }
+
+    for peer in peers:
+        pl.semaphore_signal(barrier, inc=1, device_id=where_is(*peer), device_id_type=MESH)
+
+    lane = lax.broadcasted_iota(jnp.int32, (rows_here, weights.shape[2]), 1)
+    dense = jnp.zeros((rows_here, weights.shape[2]), jnp.float32)
+    for k in range(expert_choice.shape[1]):
+        dense = dense + jnp.where(lane == expert_choice[:, k : k + 1], route_weight[:, k : k + 1], 0.0)
+    own_block = h * req_count + r
+    weights[own_block] = jnp.concatenate(
+        [dense, jnp.zeros((ROW_TILE - rows_here, weights.shape[2]), jnp.float32)], axis=0
+    )
+
+    sent = []
+
+    def send(source, target, kr, kh, kp):
+        at = len(sent)
+        copy = pltpu.make_async_remote_copy(
+            src_ref=source,
+            dst_ref=target,
+            send_sem=send_sem.at[at],
+            recv_sem=recv_sem.at[at],
+            device_id=where_is(kr, kh, kp),
+            device_id_type=MESH,
+        )
+        copy.start()
+        sent.append(copy)
+        return copy
+
+    loads[0].wait()
+    for k in range(moves):
+        leaving[k] = cache[leave_slots[k]]
+    pl.semaphore_wait(barrier, len(peers))
+    pages = send(leaving, arrived, 0, 0, 1)
+    weight_copies = [
+        send(weights.at[own_block], weights.at[own_block], kr, kh, 0)
+        for kr in range(req_count)
+        for kh in range(head_count)
+        if kr or kh
+    ]
+    loads[1].wait()
+    loads[2].wait()
+    pages.wait_recv()
+
+    def gather(b, carry):
+        slot = page_table[b]
+        which, moved = jnp.int32(0), jnp.int32(0)
+        for k in range(moves):
+            hit = arrive_slots[k] == slot
+            which = jnp.where(hit, k, which)
+            moved = jnp.where(hit, 1, moved)
+        flag = jnp.full((page, 2 * head_dim), moved, jnp.int32) > 0
+        kept = cache[slot].astype(jnp.float32)
+        swapped_in = arrived[which].astype(jnp.float32)
+        context[b] = jnp.where(flag, swapped_in, kept).astype(jnp.bfloat16)
+        return carry
+
+    lax.fori_loop(0, batch, gather, 0, unroll=8)
+
+    tile_rows = group_size * ROW_TILE
+    score_scale = head_dim ** (-0.5)
+    for c in range(chunks):
+        base = c * ROW_TILE
+        stacked = jnp.concatenate(
+            [
+                queries[base : base + ROW_TILE, g * head_dim : (g + 1) * head_dim]
+                for g in range(group_size)
+            ],
+            axis=0,
+        )
+        block = context[base : base + ROW_TILE].reshape(ROW_TILE * page, 2 * head_dim)
+        scores = (
+            lax.dot_general(
+                stacked,
+                block[:, :head_dim],
+                (((1,), (1,)), ((), ())),
+                preferred_element_type=jnp.float32,
+            )
+            * score_scale
+        )
+        shape = (ROW_TILE, ROW_TILE * page)
+        first = lax.broadcasted_iota(jnp.int32, shape, 0) * page
+        offset = lax.broadcasted_iota(jnp.int32, shape, 1) - first
+        live = (offset >= 0) & (offset < cached_length[base : base + ROW_TILE, :])
+        bias = jnp.where(live, 0.0, NEGATIVE)
+        bias = jnp.concatenate([bias] * group_size, axis=0)
+        scores = jnp.where(bias < 0.0, NEGATIVE, scores)
+        newest = fresh[base : base + ROW_TILE, :].astype(jnp.float32)
+        newest = jnp.concatenate([newest] * group_size, axis=0)
+        fresh_score = (
+            jnp.sum(stacked.astype(jnp.float32) * newest[:, :head_dim], axis=-1, keepdims=True)
+            * score_scale
+        )
+        largest = jnp.maximum(jnp.max(scores, axis=-1, keepdims=True), fresh_score)
+        raised = jnp.exp(scores - largest)
+        fresh_raised = jnp.exp(fresh_score - largest)
+        denominator = jnp.sum(raised, axis=-1, keepdims=True) + fresh_raised
+        value = jnp.dot(
+            raised.astype(jnp.bfloat16), block[:, head_dim:], preferred_element_type=jnp.float32
+        )
+        value = (value + fresh_raised * newest[:, head_dim:]) / denominator
+        level = jnp.broadcast_to(largest + jnp.log(denominator), (tile_rows, head_dim))
+        for s in range(pool_count):
+            rows = slice(s * half_heads * ROW_TILE, (s + 1) * half_heads * ROW_TILE)
+            values_out[s, c] = value[rows].astype(jnp.bfloat16)
+            level_out[s, c] = level[rows]
+    value_copy = send(values_out.at[partner], values_in, 0, 0, 1)
+    level_copy = send(level_out.at[partner], level_in, 0, 0, 1)
+
+    spread = lax.broadcasted_iota(jnp.int32, (batch, rows_here), 0) == (
+        lax.broadcasted_iota(jnp.int32, (batch, rows_here), 1) + h * rows_here
+    )
+    spread = jnp.where(p == 0, spread.astype(jnp.float32), 0.0).astype(jnp.bfloat16)
+    loads[3].wait()
+    value_copy.wait_recv()
+    level_copy.wait_recv()
+    merged = []
+    for c in range(chunks):
+        first_level, second_level = level_out[p, c], level_in[c]
+        top = jnp.maximum(first_level, second_level)
+        first_share = jnp.exp(first_level - top)
+        second_share = jnp.exp(second_level - top)
+        value = values_out[p, c].astype(jnp.float32) * first_share
+        value = value + values_in[c].astype(jnp.float32) * second_share
+        value = (value / (first_share + second_share)).astype(jnp.bfloat16)
+        merged.append(
+            jnp.concatenate(
+                [value[g * ROW_TILE : (g + 1) * ROW_TILE] for g in range(half_heads)], axis=1
+            )
+        )
+    merged = jnp.concatenate(merged, axis=0)
+    blocks = head_count * pool_count
+    for d in range(blocks):
+        columns = slice(d * col_block, (d + 1) * col_block)
+        part = jnp.dot(merged, output_weight[:, columns], preferred_element_type=jnp.float32)
+        part = part + jnp.dot(spread, residual[:, columns], preferred_element_type=jnp.float32)
+        partial_out[d] = part.astype(jnp.bfloat16)
+    partial_copies = []
+    for kh in list(range(1, head_count)) + [0]:
+        for kp in range(pool_count):
+            if kh or kp:
+                to_pool = partner if kp else p
+                to_head = head_peer(kh) if kh else h
+                partial_copies.append(
+                    send(
+                        partial_out.at[to_pool * head_count + to_head],
+                        partial_in.at[kh * pool_count + kp],
+                        0,
+                        kh,
+                        kp,
+                    )
+                )
+    mine = p * head_count + h
+    summed = partial_out[mine].astype(jnp.float32)
+    order = [kh * pool_count + kp for kh in list(range(1, head_count)) + [0] for kp in range(pool_count) if kh or kp]
+    for copy, slot in zip(partial_copies, order):
+        copy.wait_recv()
+        summed = summed + partial_in[slot].astype(jnp.float32)
+    hidden[mine, r] = summed.astype(jnp.bfloat16)
+
+    def hidden_block(at_head, at_req):
+        return hidden.at[p * head_count + at_head, at_req]
+
+    own_hidden = hidden_block(h, r)
+    req_copies = {kr: send(own_hidden, own_hidden, kr, 0, 0) for kr in range(1, req_count)}
+    head_copies, pool_copies = {}, {}
+    for kh in range(1, head_count):
+        head_copies[kh, 0] = send(own_hidden, own_hidden, 0, kh, 0)
+    pool_copies[0, 0] = send(own_hidden, own_hidden, 0, 0, 1)
+    for kr in range(1, req_count):
+        req_copies[kr].wait_recv()
+        block = hidden_block(h, req_source(kr))
+        for kh in range(1, head_count):
+            head_copies[kh, kr] = send(block, block, 0, kh, 0)
+        pool_copies[0, kr] = send(block, block, 0, 0, 1)
+
+    loads[4].wait()
+    row_count = req_count * batch
+    units = gate_up.shape[1]
+    gate = jnp.zeros((row_count, units), jnp.float32)
+    up = jnp.zeros((row_count, units), jnp.float32)
+    squares = jnp.zeros((row_count, 1), jnp.float32)
+
+    def accumulate(state, chunk):
+        gate, up, squares = state
+        x = hidden[chunk].reshape(row_count, col_block).astype(jnp.float32)
+        columns = pl.ds(pl.multiple_of(chunk * col_block, col_block), col_block)
+        scaled = (x * norm_gain[:, columns]).astype(jnp.bfloat16)
+        contract = (((1,), (1,)), ((), ()))
+        gate = gate + lax.dot_general(
+            scaled, gate_up[0, :, columns], contract, preferred_element_type=jnp.float32
+        )
+        up = up + lax.dot_general(
+            scaled, gate_up[1, :, columns], contract, preferred_element_type=jnp.float32
+        )
+        return gate, up, squares + jnp.sum(x * x, axis=-1, keepdims=True)
+
+    state = (gate, up, squares)
+    state = accumulate(state, mine)
+    for kh in range(1, head_count):
+        for kr in range(req_count):
+            head_copies[kh, kr].wait_recv()
+            block = hidden_block(head_source(kh), req_source(kr) if kr else r)
+            pool_copies[kh, kr] = send(block, block, 0, 0, 1)
+        state = accumulate(state, p * head_count + head_source(kh))
+    for kh in range(head_count):
+        for kr in range(req_count):
+            pool_copies[kh, kr].wait_recv()
+        state = accumulate(state, partner * head_count + (head_source(kh) if kh else h))
+    gate, up, squares = state
+    scale = lax.rsqrt(squares * (1.0 / width) + 1e-06)
+    gate = gate * scale
+    activated = (gate / (1.0 + jnp.exp(-gate)) * (up * scale)).astype(jnp.bfloat16)
+    place_row = lax.broadcasted_iota(jnp.int32, (ROW_TILE, row_count), 0)
+    place_col = lax.broadcasted_iota(jnp.int32, (ROW_TILE, row_count), 1)
+    for copy in weight_copies:
+        copy.wait_recv()
+    for to_head in range(head_count):
+        placing = jnp.concatenate(
+            [
+                (
+                    (place_row + (to_req * batch + to_head * rows_here) == place_col)
+                    & (place_row < rows_here)
+                )
+                .astype(jnp.float32)
+                .astype(jnp.bfloat16)
+                for to_req in range(req_count)
+            ],
+            axis=0,
+        )
+        active[to_head] = jnp.dot(placing, activated, preferred_element_type=jnp.float32).astype(
+            jnp.bfloat16
+        )
+    loads[5].wait()
+    expert = r * head_count + h
+    group_rows = req_count * ROW_TILE
+
+    def expert_part(to_head, side):
+        table = weights[pl.ds(to_head * req_count, req_count)].reshape(group_rows, -1)
+        spot = lax.broadcasted_iota(jnp.int32, table.shape, 1)
+        weight = jnp.sum(jnp.where(spot == expert, table, 0.0), axis=-1, keepdims=True)
+        columns = pl.ds(pl.multiple_of(side * half, half), half)
+        value = jnp.dot(
+            active[to_head], down_weight[:, columns], preferred_element_type=jnp.float32
+        )
+        return value * weight
+
+    turn = list(range(1, head_count)) + [0]
+    swap_copies = {}
+    for kh in turn:
+        pool_out[kh] = expert_part(head_peer(kh) if kh else h, partner).astype(jnp.bfloat16)
+        swap_copies[kh] = send(pool_out.at[kh], pool_in.at[kh], 0, 0, 1)
+    for kh in turn:
+        own_part[kh] = expert_part(head_peer(kh) if kh else h, p)
+    back_copies = []
+    for kh in turn:
+        swap_copies[kh].wait_recv()
+        both = own_part[kh] + pool_in[kh].astype(jnp.float32)
+        if kh:
+            head_out[kh - 1] = both.astype(jnp.bfloat16)
+            back_copies.append(send(head_out.at[kh - 1], head_in.at[kh - 1], 0, kh, 0))
+    for kh, copy in enumerate(back_copies):
+        copy.wait_recv()
+        both = both + head_in[kh].astype(jnp.float32)
+    totals[...] = both.reshape(req_count, ROW_TILE, half)
+    last_copies = []
+    for kr in range(1, req_count):
+        req_out[kr - 1] = totals[req_peer(kr)].astype(jnp.bfloat16)
+        last_copies.append(send(req_out.at[kr - 1], req_in.at[kr - 1], kr, 0, 0))
+    pick = lax.broadcasted_iota(jnp.int32, (ROW_TILE, batch), 1) == (
+        lax.broadcasted_iota(jnp.int32, (ROW_TILE, batch), 0) + h * rows_here
+    )
+    pick = pick.astype(jnp.float32).astype(jnp.bfloat16)
+    stream = jnp.concatenate(
+        [
+            jnp.dot(pick, hidden[p * head_count + c, r], preferred_element_type=jnp.float32)
+            for c in range(head_count)
+        ],
+        axis=1,
+    )
+    total = stream + totals[r]
+    for kr, copy in enumerate(last_copies):
+        copy.wait_recv()
+        total = total + req_in[kr].astype(jnp.float32)
+    decoded[...] = total[:rows_here].astype(jnp.bfloat16)
+    for copy in sent:
+        copy.wait_send()
+
+
+def local(*arguments):
+    queries, new_entries, cache_pages, page_table = arguments[:4]
+    residual, expert_choice = arguments[7], arguments[10]
+    rows_here = residual.shape[0]
+    expert_count = lax.axis_size("req") * lax.axis_size("head")
+    capacity = max(
+        2,
+        min(
+            rows_here,
+            (2 * rows_here * expert_choice.shape[1] + expert_count - 1) // expert_count,
+        ),
+    )
+    fits = (
+        capacity == rows_here
+        and rows_here <= ROW_TILE
+        and expert_count <= 128
+        and cache_pages.shape[0] == 1
+        and page_table.shape[2] == 1
+        and cache_pages.shape[2] == ROW_TILE
+        and queries.shape[0] % ROW_TILE == 0
+        and queries.shape[0] == rows_here * lax.axis_size("head")
+        and lax.axis_size("pool") == 2
+        and new_entries.shape[1] == 2
+        and arguments[12].shape[0] == 1
+    )
+    if not fits:
+        return local_routed(*arguments)
+    return local_dense(*arguments)
+
+
+def local_dense(
+    queries,
+    new_entries,
+    cache_pages,
+    page_table,
+    cached_length,
+    leave_slots,
+    arrive_slots,
+    residual,
+    norm_gain,
+    output_weight,
+    expert_choice,
+    route_weight,
+    gate_up,
+    down_weight,
+):
+    reqs, heads, pools = lax.axis_size("req"), lax.axis_size("head"), lax.axis_size("pool")
+    batch = queries.shape[0]
+    rows_here, width = residual.shape
+    slots, page, entry = cache_pages.shape[1:]
+    head_dim = entry // 2
+    group_size = queries.shape[1] // head_dim
+    moves = leave_slots.shape[0]
+    fresh = new_entries.reshape(batch, -1, entry).transpose(1, 0, 2)
+    col_block = width // (heads * pools)
+    half = width // pools
+    chunks = batch // ROW_TILE
+    half_rows = group_size // pools * ROW_TILE
+    group_rows = reqs * ROW_TILE
+    units = gate_up.shape[2]
+    copies = (
+        1
+        + (reqs * heads - 1)
+        + 2
+        + (heads * pools - 1)
+        + (reqs - 1)
+        + reqs * (heads - 1)
+        + reqs * heads
+        + heads
+        + (heads - 1)
+        + (reqs - 1)
+    )
+    smem = pl.BlockSpec(memory_space=pltpu.SMEM)
+    vmem = pl.BlockSpec(memory_space=pltpu.VMEM)
+    hbm = pl.BlockSpec(memory_space=pl.ANY)
+    narrow, full = jnp.bfloat16, jnp.float32
+    return pl.pallas_call(
+        functools.partial(layer_kernel, reqs, heads, pools),
+        out_shape=jax.ShapeDtypeStruct((rows_here, half), narrow),
+        in_specs=[smem] * 3 + [vmem] * 5 + [hbm] * 6,
+        out_specs=vmem,
+        scratch_shapes=[
+            pltpu.VMEM(queries.shape, narrow),
+            pltpu.VMEM(fresh.shape[1:], narrow),
+            pltpu.VMEM((slots, page, entry), narrow),
+            pltpu.VMEM(output_weight.shape, narrow),
+            pltpu.VMEM(gate_up.shape[1:], narrow),
+            pltpu.VMEM(down_weight.shape[1:], narrow),
+            pltpu.VMEM((moves, page, entry), narrow),
+            pltpu.VMEM((moves, page, entry), narrow),
+            pltpu.VMEM((batch, page, entry), narrow),
+            pltpu.VMEM((heads * reqs, ROW_TILE, 128), full),
+            pltpu.VMEM((pools, chunks, half_rows, head_dim), narrow),
+            pltpu.VMEM((chunks, half_rows, head_dim), narrow),
+            pltpu.VMEM((pools, chunks, half_rows, head_dim), full),
+            pltpu.VMEM((chunks, half_rows, head_dim), full),
+            pltpu.VMEM((heads * pools, batch, col_block), narrow),
+            pltpu.VMEM((heads * pools, batch, col_block), narrow),
+            pltpu.VMEM((heads * pools, reqs, batch, col_block), narrow),
+            pltpu.VMEM((heads, group_rows, units), narrow),
+            pltpu.VMEM((heads, group_rows, half), full),
+            pltpu.VMEM((heads, group_rows, half), narrow),
+            pltpu.VMEM((heads, group_rows, half), narrow),
+            pltpu.VMEM((heads - 1, group_rows, half), narrow),
+            pltpu.VMEM((heads - 1, group_rows, half), narrow),
+            pltpu.VMEM((reqs, ROW_TILE, half), full),
+            pltpu.VMEM((reqs - 1, ROW_TILE, half), narrow),
+            pltpu.VMEM((reqs - 1, ROW_TILE, half), narrow),
+            pltpu.SemaphoreType.DMA((6,)),
+            pltpu.SemaphoreType.DMA((copies,)),
+            pltpu.SemaphoreType.DMA((copies,)),
+        ],
+        compiler_params=pltpu.CompilerParams(
+            collective_id=0, has_side_effects=True, vmem_limit_bytes=56 * 1024 * 1024
+        ),
+        name="layer",
+    )(
+        page_table.reshape(-1),
+        leave_slots,
+        arrive_slots,
+        cached_length,
+        expert_choice,
+        route_weight,
+        residual,
+        norm_gain.reshape(1, -1),
+        queries,
+        fresh,
+        cache_pages,
+        output_weight,
+        gate_up,
+        down_weight,
+    )
+
+
 def solution(mesh):
     return jax.shard_map(
         local,

time: 160 us -> 47.2 us (0.30)
  waiting for transfers between devices: 78.1 us -> 0 us
  Pallas kernels: 0 us -> 40 us
  blocking collectives: 36.1 us -> 0 us
  between operations: 13.6 us -> 0.01 us
  matrix products: 9.56 us -> 0 us
  starting transfers between devices: 7.33 us -> 0 us
  other arithmetic: 4.95 us -> 0 us
  local copies, waits for them, and re-layouts: 10 us -> 6.86 us
    psum x1 -> x0, waiting for transfers between devices: 56.1 us -> none  [local(): lax.psum(partial_value.astype(jnp.bfloat16), ('head', 'pool'))]
    pallas_call x0 -> x1, Pallas kernels: none -> 40 us  [local_dense(): pl.pallas_call(functools.partial(layer_kernel, reqs, heads, pools), out_s...]
    all_to_all x1 -> x0, blocking collectives: 30.5 us -> none  [local(): lax.all_to_all(outgoing_rows, ('req', 'head'), split_axis=0, concat_axis=...]
    all_to_all x1 -> x0, waiting for transfers between devices: 15.5 us -> none  [local(): lax.all_to_all(column_sum, ('req', 'head'), split_axis=0, concat_axis=0,...]
    dot_general x9 -> x0, matrix products: 9.56 us -> none  [the longest x1 2.38 us: local(): jnp.dot(activated, down_weight[0], preferred_element_type=jnp.float32)]
    all_to_all x1 -> x0, starting transfers between devices: 6.73 us -> none  [local(): lax.all_to_all(column_sum, ('req', 'head'), split_axis=0, concat_axis=0,...]
    reduce_scatter x1 -> x0, waiting for transfers between devices: 6.55 us -> none  [local(): lax.psum_scatter(part_sum.astype(jnp.bfloat16), 'pool', scatter_dimension...]
    all_gather x3 -> x0, blocking collectives: 5.63 us -> none  [combined_all(): lax.all_gather(a.astype(kind), axis)]
  transfers between devices with their start and end apart: 4 -> 0, of which waited for: 3 -> 0; matrix products, arithmetic and copies ran while one was open for 3% -> 0% of each run, Pallas kernels for 0% -> 0%
where the time goes in v1:
time: 47.2 us; the launch traced here: 46.8 us
  Pallas kernels  40 us (85%)
  local copies, waits for them, and re-layouts  6.86 us (15%)
    pallas_call x1, Pallas kernels, local_dense(): pl.pallas_call(functools.partial(layer_kernel, reqs, heads, pools), out_s...  40 us
    unnamed x5, local copies, waits for them, and re-layouts  6.86 us

profile of v1, /device:TPU:0, one launch (start us, length us, event | category | flops | bytes accessed | tf_op | source)
XLA Modules:
  0.0 46.8 jit_solution(16917057508107939821)
XLA Ops:
  0.0 1.4 %copy.17.expert_choice = s32[12,8]{1,0:T(8,128)} copy(s32[12,8]{0,1:T(8,128)} %param.24) | data formatting | bytes 768 | tf_op args[10]
  1.4 1.4 %copy.18.route_weight = f32[12,8]{1,0:T(8,128)} copy(f32[12,8]{0,1:T(8,128)} %param.25) | data formatting | bytes 768 | tf_op args[11]
  2.7 1.3 %copy.16.cached_length = s32[48,1]{1,0:T(8,128)} copy(s32[48,1]{0,1:T(1,128)} %param.18) | data formatting | bytes 384 | tf_op args[4]
  4.1 1.4 %copy.20 = bf16[48,2,1,256]{3,0,1,2:T(8,128)(2,1)} copy(bf16[48,2,1,256]{3,1,2,0:T(2,128)(2,1)} %param.15) | data formatting | bytes 98304 | tf_op args[1]
  5.5 40.0 %layer.1 = bf16[12,1024]{1,0:T(8,128)(2,1)} custom-call(s32[48]{0:T(128)} %bitcast.9, s32[4]{0:T(128)} %leave_slots.1, s32[4]{0:T(128)} %arrive_slots.1, s32[48,1]{1,0:T(8,128)} %copy.16.cached_length, s32[12,8]{1,0:T(8,128)} %copy.17.expert_choice, f32[12,8]{1,0:T(8,128)} %copy.18.route_weight, bf16[12,2048]{1,0:T(8,128)(2,1)} %residual.1, ...), custom_call_target="tpu_custom_call" | custom-call | tf_op jit(solution)/shard_map/layer/pallas_call | solution.py:639
  45.5 1.4 %copy.22 = bf16[12,1024]{1,0:T(8,128)(2,1)} copy(bf16[12,1024]{1,0:T(8,128)(2,1)} %layer.1) | data formatting | bytes 49152

commit v2 on v1

--- a/solution.py
+++ b/solution.py
@@ -233,7 +233,7 @@
             (
                 (cache_hbm.at[0], cache),
                 (queries_hbm, queries),
-                (fresh_hbm.at[p], fresh),
+                (fresh_hbm, fresh),
                 (output_weight_hbm, output_weight),
                 (gate_up_hbm.at[0], gate_up),
                 (down_weight_hbm.at[0], down_weight),
@@ -275,13 +275,14 @@
     for peer in peers:
         pl.semaphore_signal(barrier, inc=1, device_id=where_is(*peer), device_id_type=MESH)
 
-    lane = lax.broadcasted_iota(jnp.int32, (rows_here, weights.shape[2]), 1)
-    dense = jnp.zeros((rows_here, weights.shape[2]), jnp.float32)
-    for k in range(expert_choice.shape[1]):
-        dense = dense + jnp.where(lane == expert_choice[:, k : k + 1], route_weight[:, k : k + 1], 0.0)
+    experts = weights.shape[1]
+    named = lax.broadcasted_iota(jnp.int32, (experts, rows_here), 0)
+    dense = jnp.zeros((experts, rows_here), jnp.float32)
+    for k in range(expert_choice.shape[0]):
+        dense = dense + jnp.where(named == expert_choice[k : k + 1, :], route_weight[k : k + 1, :], 0.0)
     own_block = h * req_count + r
     weights[own_block] = jnp.concatenate(
-        [dense, jnp.zeros((ROW_TILE - rows_here, weights.shape[2]), jnp.float32)], axis=0
+        [dense, jnp.zeros((experts, weights.shape[2] - rows_here), jnp.float32)], axis=1
     )
 
     sent = []
@@ -331,6 +332,15 @@
     lax.fori_loop(0, batch, gather, 0, unroll=8)
 
     tile_rows = group_size * ROW_TILE
+    here = lax.broadcasted_iota(jnp.int32, (batch, batch), 0)
+    there = lax.broadcasted_iota(jnp.int32, (batch, batch), 1)
+    lengths = jnp.where(here == there, cached_length[...].astype(jnp.float32), 0.0)
+    lengths = jnp.sum(lengths, axis=-1, keepdims=True)
+    to_entry = lax.broadcasted_iota(jnp.int32, (ROW_TILE, 2 * ROW_TILE), 1) == (
+        2 * lax.broadcasted_iota(jnp.int32, (ROW_TILE, 2 * ROW_TILE), 0) + p
+    )
+    to_entry = to_entry.astype(jnp.float32).astype(jnp.bfloat16)
+    to_entry = jnp.concatenate([to_entry] * group_size, axis=0)
     score_scale = head_dim ** (-0.5)
     for c in range(chunks):
         base = c * ROW_TILE
@@ -354,12 +364,14 @@
         shape = (ROW_TILE, ROW_TILE * page)
         first = lax.broadcasted_iota(jnp.int32, shape, 0) * page
         offset = lax.broadcasted_iota(jnp.int32, shape, 1) - first
-        live = (offset >= 0) & (offset < cached_length[base : base + ROW_TILE, :])
+        live = (offset >= 0) & (
+            offset.astype(jnp.float32) < lengths[base : base + ROW_TILE]
+        )
         bias = jnp.where(live, 0.0, NEGATIVE)
         bias = jnp.concatenate([bias] * group_size, axis=0)
         scores = jnp.where(bias < 0.0, NEGATIVE, scores)
-        newest = fresh[base : base + ROW_TILE, :].astype(jnp.float32)
-        newest = jnp.concatenate([newest] * group_size, axis=0)
+        newest = fresh[base : base + ROW_TILE].reshape(2 * ROW_TILE, 2 * head_dim)
+        newest = jnp.dot(to_entry, newest, preferred_element_type=jnp.float32)
         fresh_score = (
             jnp.sum(stacked.astype(jnp.float32) * newest[:, :head_dim], axis=-1, keepdims=True)
             * score_scale
@@ -506,12 +518,19 @@
         )
     loads[5].wait()
     expert = r * head_count + h
-    group_rows = req_count * ROW_TILE
+    diagonal = lax.broadcasted_iota(jnp.int32, (ROW_TILE, weights.shape[2]), 0) == (
+        lax.broadcasted_iota(jnp.int32, (ROW_TILE, weights.shape[2]), 1)
+    )
 
     def expert_part(to_head, side):
-        table = weights[pl.ds(to_head * req_count, req_count)].reshape(group_rows, -1)
-        spot = lax.broadcasted_iota(jnp.int32, table.shape, 1)
-        weight = jnp.sum(jnp.where(spot == expert, table, 0.0), axis=-1, keepdims=True)
+        weight = jnp.concatenate(
+            [
+                jnp.where(diagonal, weights[to_head * req_count + k, pl.ds(expert, 1), :], 0.0)
+                for k in range(req_count)
+            ],
+            axis=0,
+        )
+        weight = jnp.sum(weight, axis=-1, keepdims=True)
         columns = pl.ds(pl.multiple_of(side * half, half), half)
         value = jnp.dot(
             active[to_head], down_weight[:, columns], preferred_element_type=jnp.float32
@@ -530,12 +549,13 @@
         swap_copies[kh].wait_recv()
         both = own_part[kh] + pool_in[kh].astype(jnp.float32)
         if kh:
-            head_out[kh - 1] = both.astype(jnp.bfloat16)
+            head_out[kh - 1] = both.reshape(req_count, ROW_TILE, half)[:, :rows_here].astype(jnp.bfloat16)
             back_copies.append(send(head_out.at[kh - 1], head_in.at[kh - 1], 0, kh, 0))
+    both = both.reshape(req_count, ROW_TILE, half)[:, :rows_here]
     for kh, copy in enumerate(back_copies):
         copy.wait_recv()
         both = both + head_in[kh].astype(jnp.float32)
-    totals[...] = both.reshape(req_count, ROW_TILE, half)
+    totals[...] = both
     last_copies = []
     for kr in range(1, req_count):
         req_out[kr - 1] = totals[req_peer(kr)].astype(jnp.bfloat16)
@@ -551,11 +571,11 @@
         ],
         axis=1,
     )
-    total = stream + totals[r]
+    total = stream[:rows_here] + totals[r]
     for kr, copy in enumerate(last_copies):
         copy.wait_recv()
         total = total + req_in[kr].astype(jnp.float32)
-    decoded[...] = total[:rows_here].astype(jnp.bfloat16)
+    decoded[...] = total.astype(jnp.bfloat16)
     for copy in sent:
         copy.wait_send()
 
@@ -613,7 +633,7 @@
     head_dim = entry // 2
     group_size = queries.shape[1] // head_dim
     moves = leave_slots.shape[0]
-    fresh = new_entries.reshape(batch, -1, entry).transpose(1, 0, 2)
+    fresh = new_entries.reshape(batch, -1, entry)
     col_block = width // (heads * pools)
     half = width // pools
     chunks = batch // ROW_TILE
@@ -643,7 +663,7 @@
         out_specs=vmem,
         scratch_shapes=[
             pltpu.VMEM(queries.shape, narrow),
-            pltpu.VMEM(fresh.shape[1:], narrow),
+            pltpu.VMEM(fresh.shape, narrow),
             pltpu.VMEM((slots, page, entry), narrow),
             pltpu.VMEM(output_weight.shape, narrow),
             pltpu.VMEM(gate_up.shape[1:], narrow),
@@ -651,7 +671,7 @@
             pltpu.VMEM((moves, page, entry), narrow),
             pltpu.VMEM((moves, page, entry), narrow),
             pltpu.VMEM((batch, page, entry), narrow),
-            pltpu.VMEM((heads * reqs, ROW_TILE, 128), full),
+            pltpu.VMEM((heads * reqs, -(-reqs * heads // 8) * 8, 128), full),
             pltpu.VMEM((pools, chunks, half_rows, head_dim), narrow),
             pltpu.VMEM((chunks, half_rows, head_dim), narrow),
             pltpu.VMEM((pools, chunks, half_rows, head_dim), full),
@@ -663,11 +683,11 @@
             pltpu.VMEM((heads, group_rows, half), full),
             pltpu.VMEM((heads, group_rows, half), narrow),
             pltpu.VMEM((heads, group_rows, half), narrow),
-            pltpu.VMEM((heads - 1, group_rows, half), narrow),
-            pltpu.VMEM((heads - 1, group_rows, half), narrow),
-            pltpu.VMEM((reqs, ROW_TILE, half), full),
-            pltpu.VMEM((reqs - 1, ROW_TILE, half), narrow),
-            pltpu.VMEM((reqs - 1, ROW_TILE, half), narrow),
+            pltpu.VMEM((heads - 1, reqs, rows_here, half), narrow),
+            pltpu.VMEM((heads - 1, reqs, rows_here, half), narrow),
+            pltpu.VMEM((reqs, rows_here, half), full),
+            pltpu.VMEM((reqs - 1, rows_here, half), narrow),
+            pltpu.VMEM((reqs - 1, rows_here, half), narrow),
             pltpu.SemaphoreType.DMA((6,)),
             pltpu.SemaphoreType.DMA((copies,)),
             pltpu.SemaphoreType.DMA((copies,)),
@@ -680,9 +700,9 @@
         page_table.reshape(-1),
         leave_slots,
         arrive_slots,
-        cached_length,
-        expert_choice,
-        route_weight,
+        cached_length.T,
+        expert_choice.T,
+        route_weight.T,
         residual,
         norm_gain.reshape(1, -1),
         queries,

time: 47.2 us -> 41.8 us (0.89)
  local copies, waits for them, and re-layouts: 6.86 us -> 1.38 us
    unnamed x5 -> x1, local copies, waits for them, and re-layouts: 6.86 us -> 1.38 us
where the time goes in v2:
time: 41.8 us; the launch traced here: 41.5 us
  Pallas kernels  40.1 us (96%)
  local copies, waits for them, and re-layouts  1.38 us (3%)
    pallas_call x1, Pallas kernels, local_dense(): pl.pallas_call(functools.partial(layer_kernel, reqs, heads, pools), out_s...  40.1 us
    unnamed x1, local copies, waits for them, and re-layouts  1.38 us

profile of v2, /device:TPU:0, one launch (start us, length us, event | category | flops | bytes accessed | tf_op | source)
XLA Modules:
  0.0 41.5 jit_solution(15676111725587437996)
XLA Ops:
  0.0 40.1 %layer.1 = bf16[12,1024]{1,0:T(8,128)(2,1)} custom-call(s32[48]{0:T(128)} %bitcast.10, s32[4]{0:T(128)} %leave_slots.1, s32[4]{0:T(128)} %arrive_slots.1, s32[1,48]{1,0:T(1,128)} %bitcast.11, s32[8,12]{1,0:T(8,128)} %bitcast.8, f32[8,12]{1,0:T(8,128)} %bitcast.9, bf16[12,2048]{1,0:T(8,128)(2,1)} %residual.1, f32[1,2048]{1,0:T(1,128)} %bitcast.7, ...), custom_call_target="tpu_custom_call" | custom-call | tf_op jit(solution)/shard_map/layer/pallas_call | solution.py:659
  40.2 1.4 %copy.16 = bf16[12,1024]{1,0:T(8,128)(2,1)} copy(bf16[12,1024]{1,0:T(8,128)(2,1)} %layer.1) | data formatting | bytes 49152

commit v3 on v2

--- a/solution.py
+++ b/solution.py
@@ -262,7 +262,7 @@
         for kr in range(req_count)
         for kh in range(head_count)
         for kp in range(pool_count)
-        if (kr, kh, kp) != (0, 0, 0) and (kp == 0 or kr == 0)
+        if (kr, kh, kp) != (0, 0, 0) and (kr > 0) + (kh > 0) + (kp > 0) == 1
     ]
 
     def where_is(kr, kh, kp):
@@ -307,10 +307,7 @@
     pl.semaphore_wait(barrier, len(peers))
     pages = send(leaving, arrived, 0, 0, 1)
     weight_copies = [
-        send(weights.at[own_block], weights.at[own_block], kr, kh, 0)
-        for kr in range(req_count)
-        for kh in range(head_count)
-        if kr or kh
+        send(weights.at[own_block], weights.at[own_block], kr, 0, 0) for kr in range(1, req_count)
     ]
     loads[1].wait()
     loads[2].wait()
@@ -391,6 +388,10 @@
             level_out[s, c] = level[rows]
     value_copy = send(values_out.at[partner], values_in, 0, 0, 1)
     level_copy = send(level_out.at[partner], level_in, 0, 0, 1)
+    for copy in weight_copies:
+        copy.wait_recv()
+    own_line = weights.at[pl.ds(h * req_count, req_count)]
+    weight_copies = [send(own_line, own_line, 0, kh, 0) for kh in range(1, head_count)]
 
     spread = lax.broadcasted_iota(jnp.int32, (batch, rows_here), 0) == (
         lax.broadcasted_iota(jnp.int32, (batch, rows_here), 1) + h * rows_here
@@ -488,10 +489,13 @@
             block = hidden_block(head_source(kh), req_source(kr) if kr else r)
             pool_copies[kh, kr] = send(block, block, 0, 0, 1)
         state = accumulate(state, p * head_count + head_source(kh))
-    for kh in range(head_count):
         for kr in range(req_count):
-            pool_copies[kh, kr].wait_recv()
-        state = accumulate(state, partner * head_count + (head_source(kh) if kh else h))
+            pool_copies[kh - 1, kr].wait_recv()
+        state = accumulate(state, partner * head_count + (head_source(kh - 1) if kh > 1 else h))
+    last = head_count - 1
+    for kr in range(req_count):
+        pool_copies[last, kr].wait_recv()
+    state = accumulate(state, partner * head_count + (head_source(last) if last else h))
     gate, up, squares = state
     scale = lax.rsqrt(squares * (1.0 / width) + 1e-06)
     gate = gate * scale
@@ -544,21 +548,33 @@
         swap_copies[kh] = send(pool_out.at[kh], pool_in.at[kh], 0, 0, 1)
     for kh in turn:
         own_part[kh] = expert_part(head_peer(kh) if kh else h, p)
-    back_copies = []
     for kh in turn:
         swap_copies[kh].wait_recv()
         both = own_part[kh] + pool_in[kh].astype(jnp.float32)
+        both = both.reshape(req_count, ROW_TILE, half)[:, :rows_here]
         if kh:
-            head_out[kh - 1] = both.reshape(req_count, ROW_TILE, half)[:, :rows_here].astype(jnp.bfloat16)
-            back_copies.append(send(head_out.at[kh - 1], head_in.at[kh - 1], 0, kh, 0))
-    both = both.reshape(req_count, ROW_TILE, half)[:, :rows_here]
-    for kh, copy in enumerate(back_copies):
-        copy.wait_recv()
-        both = both + head_in[kh].astype(jnp.float32)
-    totals[...] = both
+            head_out[kh - 1] = both.astype(jnp.bfloat16)
+        else:
+            totals[...] = both
+    back_copies = {}
+    for kr in list(range(1, req_count)) + [0]:
+        to_req = req_peer(kr) if kr else r
+        for kh in range(1, head_count):
+            back_copies[kh, kr] = send(
+                head_out.at[kh - 1, to_req], head_in.at[kh - 1, to_req], 0, kh, 0
+            )
+
+    def back_sum(kr):
+        to_req = req_peer(kr) if kr else r
+        total = totals[to_req]
+        for kh in range(1, head_count):
+            back_copies[kh, kr].wait_recv()
+            total = total + head_in[kh - 1, to_req].astype(jnp.float32)
+        return total
+
     last_copies = []
     for kr in range(1, req_count):
-        req_out[kr - 1] = totals[req_peer(kr)].astype(jnp.bfloat16)
+        req_out[kr - 1] = back_sum(kr).astype(jnp.bfloat16)
         last_copies.append(send(req_out.at[kr - 1], req_in.at[kr - 1], kr, 0, 0))
     pick = lax.broadcasted_iota(jnp.int32, (ROW_TILE, batch), 1) == (
         lax.broadcasted_iota(jnp.int32, (ROW_TILE, batch), 0) + h * rows_here
@@ -571,7 +587,7 @@
         ],
         axis=1,
     )
-    total = stream[:rows_here] + totals[r]
+    total = stream[:rows_here] + back_sum(0)
     for kr, copy in enumerate(last_copies):
         copy.wait_recv()
         total = total + req_in[kr].astype(jnp.float32)
@@ -642,14 +658,15 @@
     units = gate_up.shape[2]
     copies = (
         1
-        + (reqs * heads - 1)
+        + (reqs - 1)
+        + (heads - 1)
         + 2
         + (heads * pools - 1)
         + (reqs - 1)
         + reqs * (heads - 1)
         + reqs * heads
         + heads
-        + (heads - 1)
+        + (heads - 1) * reqs
         + (reqs - 1)
     )
     smem = pl.BlockSpec(memory_space=pltpu.SMEM)

time: 41.8 us -> 39.7 us (0.950)
  Pallas kernels: 40.1 us -> 38.1 us
    pallas_call x1, Pallas kernels: 40.1 us -> 38.1 us  [local_dense(): pl.pallas_call(functools.partial(layer_kernel, reqs, heads, pools), out_s...]
where the time goes in v3:
time: 39.7 us; the launch traced here: 39.5 us
  Pallas kernels  38.1 us (96%)
  local copies, waits for them, and re-layouts  1.38 us (3%)
    pallas_call x1, Pallas kernels, local_dense(): pl.pallas_call(functools.partial(layer_kernel, reqs, heads, pools), out_s...  38.1 us
    unnamed x1, local copies, waits for them, and re-layouts  1.38 us

profile of v3, /device:TPU:0, one launch (start us, length us, event | category | flops | bytes accessed | tf_op | source)
XLA Modules:
  0.0 39.5 jit_solution(13683182574512614729)
XLA Ops:
  0.0 38.1 %layer.1 = bf16[12,1024]{1,0:T(8,128)(2,1)} custom-call(s32[48]{0:T(128)} %bitcast.10, s32[4]{0:T(128)} %leave_slots.1, s32[4]{0:T(128)} %arrive_slots.1, s32[1,48]{1,0:T(1,128)} %bitcast.11, s32[8,12]{1,0:T(8,128)} %bitcast.8, f32[8,12]{1,0:T(8,128)} %bitcast.9, bf16[12,2048]{1,0:T(8,128)(2,1)} %residual.1, f32[1,2048]{1,0:T(1,128)} %bitcast.7, ...), custom_call_target="tpu_custom_call" | custom-call | tf_op jit(solution)/shard_map/layer/pallas_call | solution.py:676
  38.1 1.4 %copy.16 = bf16[12,1024]{1,0:T(8,128)(2,1)} copy(bf16[12,1024]{1,0:T(8,128)(2,1)} %layer.1) | data formatting | bytes 49152

commit v4 on v3

--- a/solution.py
+++ b/solution.py
@@ -453,7 +453,7 @@
     for kh in range(1, head_count):
         head_copies[kh, 0] = send(own_hidden, own_hidden, 0, kh, 0)
     pool_copies[0, 0] = send(own_hidden, own_hidden, 0, 0, 1)
-    for kr in range(1, req_count):
+    for kr in sorted(range(1, req_count), key=lambda k: min(k, req_count - k)):
         req_copies[kr].wait_recv()
         block = hidden_block(h, req_source(kr))
         for kh in range(1, head_count):

time: 39.7 us -> 39.5 us (level)
  no operation moved by 1% of the time
where the time goes in v4:
time: 39.5 us; the launch traced here: 39.3 us
  Pallas kernels  37.9 us (96%)
  local copies, waits for them, and re-layouts  1.38 us (3%)
    pallas_call x1, Pallas kernels, local_dense(): pl.pallas_call(functools.partial(layer_kernel, reqs, heads, pools), out_s...  37.9 us
    unnamed x1, local copies, waits for them, and re-layouts  1.38 us

profile of v4, /device:TPU:0, one launch (start us, length us, event | category | flops | bytes accessed | tf_op | source)
XLA Modules:
  0.0 39.3 jit_solution(2217089917304513936)
XLA Ops:
  0.0 37.9 %layer.1 = bf16[12,1024]{1,0:T(8,128)(2,1)} custom-call(s32[48]{0:T(128)} %bitcast.10, s32[4]{0:T(128)} %leave_slots.1, s32[4]{0:T(128)} %arrive_slots.1, s32[1,48]{1,0:T(1,128)} %bitcast.11, s32[8,12]{1,0:T(8,128)} %bitcast.8, f32[8,12]{1,0:T(8,128)} %bitcast.9, bf16[12,2048]{1,0:T(8,128)(2,1)} %residual.1, f32[1,2048]{1,0:T(1,128)} %bitcast.7, ...), custom_call_target="tpu_custom_call" | custom-call | tf_op jit(solution)/shard_map/layer/pallas_call | solution.py:676
  37.9 1.4 %copy.16 = bf16[12,1024]{1,0:T(8,128)(2,1)} copy(bf16[12,1024]{1,0:T(8,128)(2,1)} %layer.1) | data formatting | bytes 49152
